TPU v7x, 256 devices: a whole 4x4x8 slice. The times are simulated.
256 devices in a mesh: row: 16 (over x_lo, y, core), col: 16 (over z, x_hi).
Axes of the slice: x: 4 (x_hi: 2, x_lo: 2; x = x_hi * 2 + x_lo), y: 4, z: 8, core: 2. Of those that a mesh axis runs over, the one named last changes fastest.
Arguments:
- row_points: bfloat16 [16384, 64], P(('row', 'col')), may hold values from -6 to 6, as said below
- col_points: bfloat16 [131072, 64], P(('col', 'row')), may hold values from -6 to 6, as said below
- row_vectors: bfloat16 [16384, 64], P(('row', 'col')), may hold values from -1 to 1
- col_vectors: bfloat16 [131072, 64], P(('col', 'row')), may hold values from -0.375 to 0.375
- weight_in: bfloat16 [64, 512], replicated, may hold values from -0.75 to 0.75
- bias_in: float32 [512], replicated, may hold values from -3 to 3
- weight_mid: bfloat16 [512, 512], replicated, may hold values from -0.75 to 0.75
- bias_mid: float32 [512], replicated, may hold values from -3 to 3
- weight_out: bfloat16 [512, 256], replicated, may hold values from -0.75 to 0.75
- ard_scales: float32 [256], replicated, may hold values from 0.002 to 0.01
- signal_scale: float32 [1], replicated, may hold values from 0.5 to 2
Outputs:
- row_result: float32 [16384, 64], P(('row', 'col'))
- col_result: float32 [131072, 64], P(('col', 'row'))
Inputs may be any that keep to these rules, and one draw needn't show every extreme that they name: `row_points`: each row point's input lies near one of 512 centres that row and column points share; which centre is not given. `col_points`: each column point's input lies near one of the same 512 centres; which centre is not given.
All inputs are finite; a program needn't handle non-finite values.
Results may differ from a plain program's by a relative error of at most 0.0041.
Values may be sent and summed in bfloat16 or wider, within the bound.
A program may use at most 64 MiB of HBM per device.

v0:
```python
import math

import jax
import jax.numpy as jnp
from jax import lax
from jax.sharding import PartitionSpec as P


def in_one_piece(arrays, axis, dim, along):
    ends, at = ([], 0)
    for a in arrays[:-1]:
        at += a.shape[along]
        ends.append(at)
    both = jnp.concatenate(arrays, axis=along)
    return tuple(jnp.split(lax.all_gather(both, axis, axis=dim, tiled=True), ends, axis=along))


def in_blocks(value, dim, peers):
    before, after = (value.shape[:dim], value.shape[dim + 1 :])
    return jnp.moveaxis(value.reshape(*before, peers, -1, *after), dim, 0)


def sum_at_owner(value, axis, dim):
    pieces = in_blocks(value, dim, lax.axis_size(axis))
    arrived = lax.all_to_all(pieces, axis, split_axis=0, concat_axis=0, tiled=True)
    return arrived.sum(axis=0)


def embed_points(points, weight_in, bias_in, weight_mid, bias_mid, weight_out, ard_scales):
    hidden_one = jnp.tanh(
        jnp.dot(points, weight_in, preferred_element_type=jnp.float32) + bias_in
    ).astype(jnp.bfloat16)
    hidden_two = jnp.tanh(
        jnp.dot(hidden_one, weight_mid, preferred_element_type=jnp.float32) + bias_mid
    ).astype(jnp.bfloat16)
    return (
        jnp.dot(hidden_two, weight_out, preferred_element_type=jnp.float32) * jnp.sqrt(ard_scales)
    ).astype(jnp.bfloat16)


def body(
    row_points,
    col_points,
    row_vectors,
    col_vectors,
    weight_in,
    bias_in,
    weight_mid,
    bias_mid,
    weight_out,
    ard_scales,
    signal_scale,
):
    row_feats = embed_points(
        row_points, weight_in, bias_in, weight_mid, bias_mid, weight_out, ard_scales
    )
    rows_all, row_vecs_all = in_one_piece((row_feats, row_vectors), "col", 0, 1)
    row_sq = jnp.sum(jnp.square(rows_all.astype(jnp.float32)), axis=1)
    count_vecs = row_vectors.shape[1]
    row_start = jnp.zeros((rows_all.shape[0], count_vecs), jnp.float32)
    total_cols = col_points.shape[0] * lax.axis_size("row")
    initial = (row_start, jnp.zeros((total_cols, count_vecs), jnp.float32))
    col_feats = embed_points(
        col_points, weight_in, bias_in, weight_mid, bias_mid, weight_out, ard_scales
    )
    shard_part = in_one_piece((col_feats, col_vectors), "row", 0, 1)
    features = shard_part[0]
    vectors = shard_part[1]
    count_cols = features.shape[0]
    step_rows = math.gcd(count_cols, 512)

    def visit(number, state):
        row_acc, col_acc = state
        feats_now = lax.dynamic_slice_in_dim(features, number * step_rows, step_rows, 0)
        vectors_now = lax.dynamic_slice_in_dim(vectors, number * step_rows, step_rows, 0)
        squares_now = jnp.sum(jnp.square(feats_now.astype(jnp.float32)), axis=1)
        inner_prod = lax.dot_general(
            rows_all, feats_now, (((1,), (1,)), ((), ())), preferred_element_type=jnp.float32
        )
        kernel = jnp.exp(inner_prod - 0.5 * row_sq[:, None] - 0.5 * squares_now[None, :]).astype(
            jnp.bfloat16
        )
        row_acc = row_acc + jnp.dot(kernel, vectors_now, preferred_element_type=jnp.float32)
        col_part = lax.dot_general(
            kernel, row_vecs_all, (((0,), (0,)), ((), ())), preferred_element_type=jnp.float32
        )
        col_acc = lax.dynamic_update_slice_in_dim(col_acc, col_part, number * step_rows, 0)
        return (row_acc, col_acc)

    row_acc, col_acc = lax.fori_loop(0, count_cols // step_rows, visit, initial)
    col_result = sum_at_owner(col_acc, "row", 0) * signal_scale[0]
    row_result = sum_at_owner(row_acc, "col", 0) * signal_scale[0]
    return (row_result, col_result)


def solution(mesh):
    in_specs = (
        P(("row", "col"), None),
        P(("col", "row"), None),
        P(("row", "col"), None),
        P(("col", "row"), None),
        P(),
        P(),
        P(),
        P(),
        P(),
        P(),
        P(),
    )
    out_specs = (P(("row", "col"), None), P(("col", "row"), None))
    return jax.shard_map(body, mesh=mesh, in_specs=in_specs, out_specs=out_specs, check_vma=False)
```

profile of v0, /device:TPU:1, one launch (start us, length us, event | category | flops | bytes accessed | tf_op | source)
XLA Modules:
  0.0 209.1 jit_solution(17192356686006793817)
XLA Ops:
  8.0 1.2 fusion.4
  9.3 1.7 fusion.8
  11.0 0.7 pad_maximum_fusion
  12.4 45.1 %all_gather.7 = bf16[1024,320]{1,0:T(8,128)(2,1)S(1)} all-gather(bf16[64,320]{1,0:T(8,128)(2,1)S(1)} %pad_maximum_fusion.1), channel_id=1, replica_groups=mesh['row'=16,'col'=16] {'col'}, dimensions={0}, use_global_device_ids=true | all-gather | bytes 696320 | tf_op jit(solution)/shard_map/all_gather | solution.py:15
  57.5 0.8 split.17
  58.5 8.9 %all-gather.2.cloned.1.call-done = bf16[8192,320]{0,1:T(8,128)(2,1)} async-done(((bf16[512,320]{0,1:T(8,128)(2,1)}), bf16[8192,320]{0,1:T(8,128)(2,1)}) %all-gather.2.cloned.1.call-update) | async-done | bytes 5242896 | tf_op jit(solution)/shard_map/all_gather | solution.py:15
  67.4 4.6 %split.16 = bf16[8192,256]{0,1:T(8,128)(2,1)} slice(bf16[8192,320]{0,1:T(8,128)(2,1)} %all-gather.2.cloned.1.call-done), slice={[0:8192], [0:256]} | slice | bytes 8388608 | tf_op jit(solution)/shard_map/split | solution.py:15
  72.1 1.5 broadcast_in_dim.9
  73.6 71.9 %while.16 = (s32[]{:T(128)}, f32[1024,64]{0,1:T(8,128)S(1)}, f32[8192,64]{0,1:T(8,128)}, bf16[8192,256]{0,1:T(8,128)(2,1)}, bf16[1024,256]{1,0:T(8,128)(2,1)}, /...) while((s32[]{:T(128)}, f32[1024,64]{0,1:T(8,128)S(1)}, ...), condition=%wide.region_3.0_spmd.clone, body=%wide.region_1.0_spmd.clone.sunk | while | flops 404751360 | bytes 6115513 | solution.py:90
  73.6 1.0 constant_dynamic-slice_fusion.2
  74.9 1.7 exponential_convert_fusion.2
  76.6 1.1 convolution_dynamic-update-slice_fusion.2
  78.1 1.0 constant_dynamic-slice_fusion.2
  79.4 1.7 exponential_convert_fusion.2
  81.1 1.1 convolution_dynamic-update-slice_fusion.2
  82.6 1.0 constant_dynamic-slice_fusion.2
  83.9 1.7 exponential_convert_fusion.2
  85.6 1.1 convolution_dynamic-update-slice_fusion.2
  87.1 1.0 constant_dynamic-slice_fusion.2
  88.4 1.7 exponential_convert_fusion.2
  90.1 1.1 convolution_dynamic-update-slice_fusion.2
  91.6 1.0 constant_dynamic-slice_fusion.2
  92.9 1.7 exponential_convert_fusion.2
  94.6 1.1 convolution_dynamic-update-slice_fusion.2
  96.1 1.0 constant_dynamic-slice_fusion.2
  97.4 1.7 exponential_convert_fusion.2
  99.1 1.1 convolution_dynamic-update-slice_fusion.2
  100.6 1.0 constant_dynamic-slice_fusion.2
  101.9 1.7 exponential_convert_fusion.2
  103.6 1.1 convolution_dynamic-update-slice_fusion.2
  105.1 1.0 constant_dynamic-slice_fusion.2
  106.4 1.7 exponential_convert_fusion.2
  108.1 1.1 convolution_dynamic-update-slice_fusion.2
  109.6 1.0 constant_dynamic-slice_fusion.2
  110.8 1.7 exponential_convert_fusion.2
  112.6 1.1 convolution_dynamic-update-slice_fusion.2
  114.0 1.0 constant_dynamic-slice_fusion.2
  115.3 1.7 exponential_convert_fusion.2
  117.1 1.1 convolution_dynamic-update-slice_fusion.2
  118.5 1.0 constant_dynamic-slice_fusion.2
  119.8 1.7 exponential_convert_fusion.2
  121.6 1.1 convolution_dynamic-update-slice_fusion.2
  123.0 1.0 constant_dynamic-slice_fusion.2
  124.3 1.7 exponential_convert_fusion.2
  126.1 1.1 convolution_dynamic-update-slice_fusion.2
  127.5 1.0 constant_dynamic-slice_fusion.2
  128.8 1.7 exponential_convert_fusion.2
  130.5 1.1 convolution_dynamic-update-slice_fusion.2
  132.0 1.0 constant_dynamic-slice_fusion.2
  133.3 1.7 exponential_convert_fusion.2
  135.0 1.1 convolution_dynamic-update-slice_fusion.2
  136.5 1.0 constant_dynamic-slice_fusion.2
  137.8 1.7 exponential_convert_fusion.2
  139.5 1.1 convolution_dynamic-update-slice_fusion.2
  141.0 1.0 constant_dynamic-slice_fusion.2
  142.3 1.7 exponential_convert_fusion.2
  144.0 1.1 convolution_dynamic-update-slice_fusion.2
  145.8 1.0 reshape.27
  146.9 8.0 %all-to-all-start = ((f32[16,1,4096]{2,1,0:T(1,128)}), f32[16,1,4096]{2,1,0:T(1,128)S(1)}, u32[]{:S(2)}, u32[]{:S(2)}) async-start(f32[16,1,4096]{2,1,0:T(1,128)} %reshape.27), calls=%async_computation | async-start | bytes 524288 | tf_op jit(solution)/shard_map/all_to_all | solution.py:25
  154.9 3.2 %copy.31 = f32[8,16,8,512]{3,2,0,1:T(8,128)} copy(f32[8,16,8,512]{3,2,1,0:T(8,128)} %bitcast.1) | data formatting | bytes 4194304 | tf_op jit(solution)/shard_map/reshape | solution.py:20
  158.0 9.4 %all-to-all-done = f32[16,1,4096]{2,1,0:T(1,128)S(1)} async-done(((f32[16,1,4096]{2,1,0:T(1,128)}), f32[16,1,4096]{2,1,0:T(1,128)S(1)}, u32[]{:S(2)}, u32[]{:S(2)}) %all-to-all-start) | async-done | bytes 262176 | tf_op jit(solution)/shard_map/all_to_all | solution.py:25
  167.5 6.4 %all-to-all-start.1 = ((f32[16,512,64]{1,2,0:T(8,128)}), f32[16,512,64]{1,2,0:T(8,128)S(1)}, u32[]{:S(2)}, u32[]{:S(2)}) async-start(f32[16,512,64]{1,2,0:T(8,128)} %bitcast.25), calls=%async_computation.1 | async-start | bytes 4194304 | tf_op jit(solution)/shard_map/all_to_all | solution.py:25
  175.0 1.3 reduce
  177.3 24.2 %all-to-all-done.1 = f32[16,512,64]{1,2,0:T(8,128)S(1)} async-done(((f32[16,512,64]{1,2,0:T(8,128)}), f32[16,512,64]{1,2,0:T(8,128)S(1)}, u32[]{:S(2)}, u32[]{:S(2)}) %all-to-all-start.1) | async-done | bytes 2097184 | tf_op jit(solution)/shard_map/all_to_all | solution.py:25
  (116 shorter events, 13.9 us)
Async XLA Ops:
  7.2 2.1 copy-start
  7.2 3.8 %copy-start.2 = (bf16[512,64]{0,1:T(8,128)(2,1)S(1)}, bf16[512,64]{0,1:T(8,128)(2,1)}, u32[]{:S(2)}) copy-start(bf16[512,64]{0,1:T(8,128)(2,1)} %param.16) | copy-start | bytes 196612
  7.2 60.2 %all-gather.2.cloned.1.call-start = ((), (), s32[]{:S(2)}) async-start(), calls=%async_computation.2 | async-start | bytes 5570560 | tf_op jit(solution)/shard_map/all_gather | solution.py:15
  8.0 3.8 %copy-start.3 = (bf16[64,512]{1,0:T(8,128)(2,1)S(1)}, bf16[64,512]{1,0:T(8,128)(2,1)}, u32[]{:S(2)}) copy-start(bf16[64,512]{1,0:T(8,128)(2,1)} %param.17) | copy-start | bytes 196612
  8.0 3.8 %copy-start.5 = (bf16[64,64]{1,0:T(8,128)(2,1)S(1)}, bf16[64,64]{1,0:T(8,128)(2,1)}, u32[]{:S(2)}) copy-start(bf16[64,64]{1,0:T(8,128)(2,1)} %param.13) | copy-start | bytes 24580
  8.0 3.8 %copy-start.6 = (f32[512]{0:T(512)S(1)}, f32[512]{0:T(512)}, u32[]{:S(2)}) copy-start(f32[512]{0:T(512)} %param.18) | copy-start | bytes 6148
  8.0 3.8 %copy-start.7 = (f32[512]{0:T(512)S(1)}, f32[512]{0:T(512)}, u32[]{:S(2)}) copy-start(f32[512]{0:T(512)} %param.20) | copy-start | bytes 6148
  9.3 2.9 %copy-start.1 = (bf16[512,256]{1,0:T(8,128)(2,1)S(1)}, bf16[512,256]{1,0:T(8,128)(2,1)}, u32[]{:S(2)}) copy-start(bf16[512,256]{1,0:T(8,128)(2,1)} %param.21) | copy-start | bytes 786436
  9.3 3.1 %copy-start.4 = (bf16[64,64]{1,0:T(8,128)(2,1)S(1)}, bf16[64,64]{1,0:T(8,128)(2,1)}, u32[]{:S(2)}) copy-start(bf16[64,64]{1,0:T(8,128)(2,1)} %param.15) | copy-start | bytes 24580
  72.1 1.5 slice-start
  146.9 20.6 %all-to-all-start = ((f32[16,1,4096]{2,1,0:T(1,128)}), f32[16,1,4096]{2,1,0:T(1,128)S(1)}, u32[]{:S(2)}, u32[]{:S(2)}) async-start(f32[16,1,4096]{2,1,0:T(1,128)} %reshape.27), calls=%async_computation | async-start | bytes 524288 | tf_op jit(solution)/shard_map/all_to_all | solution.py:25
  167.5 34.0 %all-to-all-start.1 = ((f32[16,512,64]{1,2,0:T(8,128)}), f32[16,512,64]{1,2,0:T(8,128)S(1)}, u32[]{:S(2)}, u32[]{:S(2)}) async-start(f32[16,512,64]{1,2,0:T(8,128)} %bitcast.25), calls=%async_computation.1 | async-start | bytes 4194304 | tf_op jit(solution)/shard_map/all_to_all | solution.py:25
Sparse Core Ops, SparseCore 0:
  11.9 55.4 all-gather.1
where the time goes:
time: 211 us; the launch traced here: 209 us
  matrix products  54.1 us (26%)
  blocking collectives  45.1 us (21%)
  waiting for transfers between devices  42.5 us (20%)
  local copies, waits for them, and re-layouts  31.4 us (15%)
  between operations  14.9 us (7%)
  starting transfers between devices  14.4 us (7%)
  other arithmetic  5.59 us (3%)
    all_gather x1, blocking collectives, in_one_piece(): lax.all_gather(both, axis, axis=dim, tiled=True)  45.1 us
    all_to_all x2, waiting for transfers between devices, sum_at_owner(): lax.all_to_all(pieces, axis, split_axis=0, concat_axis=0, tiled=True)  33.6 us
    dot_general x16, matrix products, visit(): lax.dot_general(rows_all, feats_now, (((1,), (1,)), ((), ())), preferred_...  27.7 us
    dot_general x16, matrix products, visit(): lax.dot_general(kernel, row_vecs_all, (((0,), (0,)), ((), ())), preferred...  17.9 us
    dynamic_slice x32, local copies, waits for them, and re-layouts, visit(): lax.dynamic_slice_in_dim(features, number * step_rows, step_rows, 0)  17.7 us
    all_to_all x2, starting transfers between devices, sum_at_owner(): lax.all_to_all(pieces, axis, split_axis=0, concat_axis=0, tiled=True)  14.4 us
    all_gather x1, waiting for transfers between devices, in_one_piece(): lax.all_gather(both, axis, axis=dim, tiled=True)  8.9 us
    split x5, local copies, waits for them, and re-layouts, in_one_piece(): jnp.split(lax.all_gather(both, axis, axis=dim, tiled=True), ends, axis=al...  5.53 us
  transfers between devices with their start and end apart: 3, of which 3 were waited for; matrix products, arithmetic and copies ran while one was open for 4% of the time, Pallas kernels for 0%

commit v1 on v0

v1 whole, which is shorter than its diff:
```python
import jax
import jax.numpy as jnp
from jax import lax
from jax.experimental import pallas as pl
from jax.experimental.pallas import tpu as pltpu
from jax.sharding import PartitionSpec as P

MESH = pl.DeviceIdType.MESH
F32 = jnp.float32
BF16 = jnp.bfloat16
LOG2E = 1.4426950408889634

NX, NY, NZ = (4, 4, 8)
Z_OFF = (0, 4, -1, 1, -2, 2, -3, 3)
Y_OFF = (0, -1, 1, 2)
X_OFF = (0, -1, 1, 2)
MINUS = {0: 0, 1: 2, 2: 4, 3: 6, 4: 1}
PLUS = {0: 0, 1: 3, 2: 5, 3: 7}


def kernel(
    rp, rv, cp, cv, w1, b1, w2, b2, w3, ard, sig,
    rout, cout,
    w1p, xr, xc, rf, fc, vrt, vct, rn, cn, pt, oc, rsend, rrecv, csend, crecv,
    y_s, y_r, z_s, z_r, x_s, x_r, p_s, p_r, rr_s, rr_r, cc_s, cc_r,
):
    row, col = (lax.axis_index("row"), lax.axis_index("col"))
    core = lax.rem(row, 2)
    y = lax.rem(lax.div(row, 2), NY)
    x = lax.div(row, 2 * NY) + 2 * lax.rem(col, 2)
    z = lax.div(col, 2)

    def dev(dx=0, dy=0, dz=0, other=0):
        px = lax.rem(x + (dx + NX), NX)
        py = lax.rem(y + (dy + NY), NY)
        pz = lax.rem(z + (dz + NZ), NZ)
        pc = 1 - core if other else core
        return (lax.rem(px, 2) * (2 * NY) + py * 2 + pc, pz * 2 + lax.div(px, 2))

    def send(src, dst, s, r, to):
        c = pltpu.make_async_remote_copy(
            src_ref=src, dst_ref=dst, send_sem=s, recv_sem=r, device_id=to, device_id_type=MESH
        )
        c.start()
        return c

    peers = [dict(dy=dy, dz=dz) for dz in Z_OFF for dy in Y_OFF if (dy, dz) != (0, 0)]
    peers += [dict(dx=dx, other=o) for o in (0, 1) for dx in X_OFF if (dx, o) != (0, 0)]
    barrier = pltpu.get_barrier_semaphore()
    for q in peers:
        pl.semaphore_signal(barrier, inc=1, device_id=dev(**q), device_id_type=MESH)

    xr[0:64, :] = jnp.concatenate([rp[...], rv[...]], axis=1)
    xc[0:512, :] = jnp.concatenate([cp[...], cv[...]], axis=1)
    w1p[0:64, :] = w1[...]
    w1p[64:128, :] = jnp.zeros_like(w1)
    pl.semaphore_wait(barrier, len(peers))

    waits = []
    ys = []
    for j, dy in enumerate(Y_OFF):
        if j:
            ys.append(
                send(xr.at[0:64], xr.at[64 * j : 64 * j + 64], y_s.at[j], y_r.at[j], dev(dy=-dy))
            )
    xs = []
    for j, dx in enumerate(X_OFF):
        if j:
            xs.append(
                send(xc.at[0:512], xc.at[512 * j : 512 * j + 512], x_s.at[j], x_r.at[j], dev(dx=-dx))
            )
    for c in ys:
        c.wait()
    for step in range(1, 5):
        now = []
        for table, d in ((MINUS, 1), (PLUS, -1)):
            if step in table:
                a, b = (table[step - 1] * 256, table[step] * 256)
                i = table[step]
                now.append(
                    send(xr.at[a : a + 256], xr.at[b : b + 256], z_s.at[i], z_r.at[i], dev(dz=d))
                )
        for c in now:
            c.wait()
    for c in xs:
        c.wait()

    def embed(raw):
        h = jnp.tanh(jnp.dot(raw, w1p[...], preferred_element_type=F32) + b1[...]).astype(BF16)
        h = jnp.tanh(jnp.dot(h, w2[...], preferred_element_type=F32) + b2[...]).astype(BF16)
        out = jnp.dot(h, w3[...], preferred_element_type=F32) * jnp.sqrt(ard[...])
        return out.astype(BF16)

    def half_sq(feats):
        f = feats.astype(F32)
        return (-0.5 * LOG2E) * jnp.sum(f * f, axis=1, keepdims=True)

    def embed_cols(i, _):
        at = pl.multiple_of(i * 512, 512)
        raw = xc[pl.ds(at, 512), :]
        fc[pl.ds(at, 512), :] = embed(raw)
        vct[:, pl.ds(at, 512)] = raw.T[64:128, :]
        return 0

    lax.fori_loop(0, 4, embed_cols, 0)
    part = [
        send(fc.at[0:2048], fc.at[2048:4096], p_s.at[0], p_r.at[0], dev(other=1)),
        send(vct.at[:, 0:2048], vct.at[:, 2048:4096], p_s.at[1], p_r.at[1], dev(other=1)),
    ]

    def embed_rows(i, _):
        at = pl.multiple_of(i * 512, 512)
        raw = xr[pl.ds(at, 512), :]
        feats = embed(raw)
        rf[pl.ds(at, 512), :] = feats
        vrt[:, pl.ds(at, 512)] = raw.T[64:128, :]
        rn[:, pl.ds(at, 512)] = jnp.broadcast_to(half_sq(feats), (512, 128)).T[0:8, :]
        return 0

    lax.fori_loop(0, 4, embed_rows, 0)
    for c in part:
        c.wait()

    def col_norms(i, _):
        at = pl.multiple_of(i * 512, 512)
        cn[pl.ds(at, 512), :] = jnp.broadcast_to(half_sq(fc[pl.ds(at, 512), :]), (512, 128))
        return 0

    lax.fori_loop(0, 8, col_norms, 0)
    oc[...] = jnp.zeros_like(oc)

    def panel(i, _):
        at = pl.multiple_of(i * 512, 512)
        inner = lax.dot_general(
            fc[...], rf[pl.ds(at, 512), :], (((1,), (1,)), ((), ())), preferred_element_type=F32
        )
        norms = jnp.concatenate([cn[...]] * 4, axis=1)
        k = jnp.exp2(inner * LOG2E + norms + rn[0:1, pl.ds(at, 512)]).astype(BF16)
        rows = jnp.dot(vct[...], k, preferred_element_type=F32)
        pt[...] = k.T
        oc[...] += jnp.dot(vrt[:, pl.ds(at, 512)], pt[...], preferred_element_type=F32)
        rt = rows.T.astype(BF16)
        for j in range(8):
            rsend[i * 8 + j] = jnp.concatenate(
                [rt[64 * j : 64 * j + 32], rt[64 * j + 32 : 64 * j + 64]], axis=1
            )
        return 0

    lax.fori_loop(0, 4, panel, 0)
    csend[...] = oc[...].astype(BF16)

    out = []
    for i, dz in enumerate(Z_OFF):
        for j, dy in enumerate(Y_OFF):
            n = 4 * i + j
            if n:
                out.append(
                    send(rsend.at[n], rrecv.at[n], rr_s.at[n], rr_r.at[n], dev(dy=dy, dz=dz))
                )
    for o in (0, 1):
        for j, dx in enumerate(X_OFF):
            n = 4 * o + j
            if n:
                out.append(
                    send(
                        csend.at[:, 512 * n : 512 * n + 512], crecv.at[n],
                        cc_s.at[n], cc_r.at[n], dev(dx=dx, other=o),
                    )
                )
    for c in out:
        c.wait()
    scale = sig[0]
    total = rsend[0].astype(F32)
    for n in range(1, 32):
        total += rrecv[n].astype(F32)
    total = total * scale
    rout[0:32, :] = total[:, 0:64]
    rout[32:64, :] = total[:, 64:128]
    total = csend[:, 0:512].astype(F32)
    for n in range(1, 8):
        total += crecv[n].astype(F32)
    cout[...] = (total * scale).T


def body(rp, cp, rv, cv, w1, b1, w2, b2, w3, ard, sig):
    vmem = pl.BlockSpec(memory_space=pltpu.VMEM)
    dma = pltpu.SemaphoreType.DMA
    return pl.pallas_call(
        kernel,
        out_shape=(jax.ShapeDtypeStruct((64, 64), F32), jax.ShapeDtypeStruct((512, 64), F32)),
        in_specs=[vmem] * 10 + [pl.BlockSpec(memory_space=pltpu.SMEM)],
        out_specs=(vmem, vmem),
        scratch_shapes=[
            pltpu.VMEM((128, 512), BF16),
            pltpu.VMEM((2048, 128), BF16),
            pltpu.VMEM((2048, 128), BF16),
            pltpu.VMEM((2048, 256), BF16),
            pltpu.VMEM((4096, 256), BF16),
            pltpu.VMEM((64, 2048), BF16),
            pltpu.VMEM((64, 4096), BF16),
            pltpu.VMEM((8, 2048), F32),
            pltpu.VMEM((4096, 128), F32),
            pltpu.VMEM((512, 4096), BF16),
            pltpu.VMEM((64, 4096), F32),
            pltpu.VMEM((32, 32, 128), BF16),
            pltpu.VMEM((32, 32, 128), BF16),
            pltpu.VMEM((64, 4096), BF16),
            pltpu.VMEM((8, 64, 512), BF16),
            dma((4,)), dma((4,)), dma((8,)), dma((8,)), dma((4,)), dma((4,)),
            dma((2,)), dma((2,)), dma((32,)), dma((32,)), dma((8,)), dma((8,)),
        ],
        compiler_params=pltpu.CompilerParams(
            collective_id=0, has_side_effects=True, vmem_limit_bytes=62 * 2**20
        ),
    )(rp, rv, cp, cv, w1, b1.reshape(1, -1), w2, b2.reshape(1, -1), w3, ard.reshape(1, -1), sig)


def solution(mesh):
    rows, cols = (P(("row", "col"), None), P(("col", "row"), None))
    in_specs = (rows, cols, rows, cols) + (P(),) * 7
    return jax.shard_map(
        body, mesh=mesh, in_specs=in_specs, out_specs=(rows, cols), check_vma=False
    )
```

time: 211 us -> 68.9 us (0.33)
  Pallas kernels: 0 us -> 62.7 us
  matrix products: 54.1 us -> 0 us
  blocking collectives: 45.1 us -> 0 us
  waiting for transfers between devices: 42.5 us -> 0 us
  local copies, waits for them, and re-layouts: 31.4 us -> 4.76 us
  starting transfers between devices: 14.4 us -> 0 us
  between operations: 14.9 us -> 1.3 us
  other arithmetic: 5.59 us -> 0 us
    pallas_call x0 -> x1, Pallas kernels: none -> 62.7 us  [body(): pl.pallas_call(kernel, out_shape=(jax.ShapeDtypeStruct((64, 64), F32), ja...]
    dot_general x52 -> x0, matrix products: 54.1 us -> none  [the longest x16 27.7 us: visit(): lax.dot_general(rows_all, feats_now, (((1,), (1,)), ((), ())), preferred_...]
    all_gather x1 -> x0, blocking collectives: 45.1 us -> none  [in_one_piece(): lax.all_gather(both, axis, axis=dim, tiled=True)]
    all_to_all x2 -> x0, waiting for transfers between devices: 33.6 us -> none  [sum_at_owner(): lax.all_to_all(pieces, axis, split_axis=0, concat_axis=0, tiled=True)]
    dynamic_slice x32 -> x0, local copies, waits for them, and re-layouts: 17.7 us -> none  [visit(): lax.dynamic_slice_in_dim(features, number * step_rows, step_rows, 0)]
    all_to_all x2 -> x0, starting transfers between devices: 14.4 us -> none  [sum_at_owner(): lax.all_to_all(pieces, axis, split_axis=0, concat_axis=0, tiled=True)]
    all_gather x1 -> x0, waiting for transfers between devices: 8.9 us -> none  [in_one_piece(): lax.all_gather(both, axis, axis=dim, tiled=True)]
    split x5 -> x0, local copies, waits for them, and re-layouts: 5.53 us -> none  [in_one_piece(): jnp.split(lax.all_gather(both, axis, axis=dim, tiled=True), ends, axis=al...]
  transfers between devices with their start and end apart: 3 -> 0, of which waited for: 3 -> 0; matrix products, arithmetic and copies ran while one was open for 4% -> 0% of each run, Pallas kernels for 0% -> 0%
where the time goes in v1:
time: 68.9 us; the launch traced here: 68.7 us
  Pallas kernels  62.7 us (91%)
  local copies, waits for them, and re-layouts  4.76 us (7%)
  between operations  1.3 us (2%)
    pallas_call x1, Pallas kernels, body(): pl.pallas_call(kernel, out_shape=(jax.ShapeDtypeStruct((64, 64), F32), ja...  62.7 us
    unnamed x7, local copies, waits for them, and re-layouts  3.03 us
    pallas_call x1, local copies, waits for them, and re-layouts, body(): pl.pallas_call(kernel, out_shape=(jax.ShapeDtypeStruct((64, 64), F32), ja...  1.73 us

profile of v1, /device:TPU:1, one launch (start us, length us, event | category | flops | bytes accessed | tf_op | source)
XLA Modules:
  0.0 68.7 jit_solution(624255674762677246)
XLA Ops:
  1.3 0.0 copy-start
  1.3 1.6 %copy.13.cp = bf16[512,64]{1,0:T(8,128)(2,1)} copy(bf16[512,64]{0,1:T(8,128)(2,1)} %param.12) | data formatting | bytes 131072 | tf_op args[1]
  2.9 0.0 copy-done
  2.9 0.8 %copy.14.cv = bf16[512,64]{1,0:T(8,128)(2,1)} copy(bf16[512,64]{0,1:T(8,128)(2,1)S(1)} %copy-done) | data formatting | bytes 131072 | tf_op args[3]
  3.7 62.7 %shard_map.122 = (f32[64,64]{1,0:T(8,128)}, f32[512,64]{1,0:T(8,128)}) custom-call(bf16[64,64]{1,0:T(8,128)(2,1)} %rp.1, bf16[64,64]{1,0:T(8,128)(2,1)} %rv.1, bf16[512,64]{1,0:T(8,128)(2,1)} %copy.13.cp, bf16[512,64]{1,0:T(8,128)(2,1)} %copy.14.cv, bf16[64,512]{1,0:T(8,128)(2,1)} %w1.1, f32[1,512]{1,0:T(1,128)} %bitcast.3, bf16[512,512]{1,0:T(8,128)(2,1)} %w2.1, ...), custom_call_target="tpu_custom_call" | custom-call | tf_op jit(solution)/shard_map/pallas_call | solution.py:188
  66.4 0.0 copy-start.1
  66.4 1.7 %copy.15 = f32[512,64]{0,1:T(8,128)} copy(f32[512,64]{1,0:T(8,128)} %get-tuple-element.3) | data formatting | bytes 262144 | tf_op jit(solution)/shard_map/pallas_call | solution.py:188
  68.1 0.0 copy-done.1
  68.1 0.6 copy.18
Async XLA Ops:
  1.3 1.6 %copy-start = (bf16[512,64]{0,1:T(8,128)(2,1)S(1)}, bf16[512,64]{0,1:T(8,128)(2,1)}, u32[]{:S(2)}) copy-start(bf16[512,64]{0,1:T(8,128)(2,1)} %param.14) | copy-start | bytes 196612
  66.4 1.7 %copy-start.1 = (f32[64,64]{1,0:T(8,128)S(1)}, f32[64,64]{1,0:T(8,128)}, u32[]{:S(2)}) copy-start(f32[64,64]{1,0:T(8,128)} %get-tuple-element.6) | copy-start | bytes 49156

commit v2 on v1

v2 whole, which is shorter than its diff:
```python
import jax
import jax.numpy as jnp
from jax import lax
from jax.experimental import pallas as pl
from jax.experimental.pallas import tpu as pltpu
from jax.sharding import PartitionSpec as P

MESH = pl.DeviceIdType.MESH
F32 = jnp.float32
BF16 = jnp.bfloat16
LOG2E = 1.4426950408889634

NX, NY, NZ = (4, 4, 8)
Z_OFF = (-3, 2, 4, 3, -2, 1, -1, 0)
Y_OFF = (0, -1, 1, 2)
X_OFF = (0, 1, -1, 2)
MINUS = {0: 7, 1: 6, 2: 4, 3: 0, 4: 2}
PLUS = {0: 7, 1: 5, 2: 1, 3: 3}


def kernel(
    rp, rv, cp, cv, w1, b1, w2, b2, w3, ard, sig,
    rout, cout,
    w1v, w2v, w3v, rpv, rvv, xr, xc, rf, fc, vrt, vct, rn, cn, pt, oc, orr,
    rsend, rrecv, csend, crecv,
    l_s, y_s, y_r, z_s, z_r, x_s, x_r, p_s, p_r, rr_s, rr_r, cc_s, cc_r,
):
    row, col = (lax.axis_index("row"), lax.axis_index("col"))
    core = lax.rem(row, 2)
    y = lax.rem(lax.div(row, 2), NY)
    x = lax.div(row, 2 * NY) + 2 * lax.rem(col, 2)
    z = lax.div(col, 2)

    def dev(dx=0, dy=0, dz=0, other=0):
        px = lax.rem(x + (dx + NX), NX)
        py = lax.rem(y + (dy + NY), NY)
        pz = lax.rem(z + (dz + NZ), NZ)
        pc = 1 - core if other else core
        return (lax.rem(px, 2) * (2 * NY) + py * 2 + pc, pz * 2 + lax.div(px, 2))

    sent = []

    def send(src, dst, s, r, to):
        c = pltpu.make_async_remote_copy(
            src_ref=src, dst_ref=dst, send_sem=s, recv_sem=r, device_id=to, device_id_type=MESH
        )
        c.start()
        sent.append(c)
        return c

    peers = [dict(other=1)] + [dict(dx=d) for d in (1, -1)]
    peers += [dict(dy=d) for d in (1, -1, 2)] + [dict(dz=d) for d in (1, -1)]
    barrier = pltpu.get_barrier_semaphore()
    for q in peers:
        pl.semaphore_signal(barrier, inc=1, device_id=dev(**q), device_id_type=MESH)

    local = []
    for i, (a, b) in enumerate(
        ((rp, rpv), (rv, rvv), (cp, xc.at[0, 0:64]), (cv, xc.at[0, 64:128]), (w1, w1v.at[0:64]),
         (w2, w2v), (w3, w3v))
    ):
        c = pltpu.make_async_copy(a, b, l_s.at[i])
        c.start()
        local.append(c)
    w1v[64:128, :] = jnp.zeros((64, 512), BF16)
    local[0].wait()
    local[1].wait()
    xr[1792:1856, :] = jnp.concatenate([rpv[...], rvv[...]], axis=1)
    local[2].wait()
    local[3].wait()
    pl.semaphore_wait(barrier, len(peers))

    ys = []
    for j, dy in enumerate(Y_OFF):
        if j:
            ys.append(
                send(
                    xr.at[1792:1856], xr.at[1792 + 64 * j : 1856 + 64 * j],
                    y_s.at[j], y_r.at[j], dev(dy=-dy),
                )
            )

    def half(slot, h):
        return xc.at[slot, :, 256 * h : 256 * h + 256]

    xs = {}
    for h in (0, 1):
        xs[2, h] = send(half(0, h), half(2, h), x_s.at[4 + h], x_r.at[4 + h], dev(dx=1))
        g = 1 - h
        xs[1, g] = send(half(0, g), half(1, g), x_s.at[2 + g], x_r.at[2 + g], dev(dx=-1))
    for c in local[4:]:
        c.wait()

    def embed(pre):
        h = jnp.tanh(pre + b1[...]).astype(BF16)
        h = jnp.tanh(jnp.dot(h, w2v[...], preferred_element_type=F32) + b2[...]).astype(BF16)
        out = jnp.dot(h, w3v[...], preferred_element_type=F32) * jnp.sqrt(ard[...])
        return out.astype(BF16)

    def half_sq(feats):
        f = feats.astype(F32)
        return (-0.5 * LOG2E) * jnp.sum(f * f, axis=1, keepdims=True)

    def embed_cols(*slots):
        points = jnp.concatenate([xc[s, 0:64, :] for s in slots], axis=1)
        pre = lax.dot_general(
            points, w1v[0:64, :], (((0,), (0,)), ((), ())), preferred_element_type=F32
        )
        feats = embed(pre)
        for i, s in enumerate(slots):
            part = feats[512 * i : 512 * i + 512]
            fc[512 * s : 512 * s + 512, :] = part
            cn[512 * s : 512 * s + 512, :] = jnp.broadcast_to(half_sq(part), (512, 128))
            vct[:, 512 * s : 512 * s + 512] = xc[s, 64:128, :]
        done = []
        for s in slots:
            lo, hi = (slice(512 * s, 512 * s + 512), slice(2048 + 512 * s, 2560 + 512 * s))
            done.append(send(fc.at[lo], fc.at[hi], p_s.at[s], p_r.at[s], dev(other=1)))
            done.append(
                send(vct.at[:, lo], vct.at[:, hi], p_s.at[4 + s], p_r.at[4 + s], dev(other=1))
            )
        return done

    def embed_rows(*slots):
        raw = jnp.concatenate([xr[256 * s : 256 * s + 256, :] for s in slots], axis=0)
        feats = embed(jnp.dot(raw, w1v[...], preferred_element_type=F32))
        values = raw.T
        norms = jnp.broadcast_to(half_sq(feats), (256 * len(slots), 128)).T
        for i, s in enumerate(slots):
            here, there = (slice(256 * i, 256 * i + 256), slice(256 * s, 256 * s + 256))
            rf[there, :] = feats[here]
            vrt[:, there] = values[64:128, here]
            rn[:, there] = norms[0:8, here]

    def z_step(step):
        now = []
        for table, d in ((MINUS, 1), (PLUS, -1)):
            if step in table:
                a, b = (table[step - 1] * 256, table[step] * 256)
                i = table[step]
                now.append(
                    send(xr.at[a : a + 256], xr.at[b : b + 256], z_s.at[i], z_r.at[i], dev(dz=d))
                )
        return now

    def arrive(copies):
        for c in copies:
            c.wait_recv()

    def panel(p, lo, hi, first_rows, first_cols):
        r = slice(512 * p, 512 * p + 512)
        inner = lax.dot_general(
            fc[lo:hi, :], rf[r, :], (((1,), (1,)), ((), ())), preferred_element_type=F32
        )
        norms = jnp.concatenate([cn[lo:hi, :]] * 4, axis=1)
        k = jnp.exp2(inner * LOG2E + norms + rn[0:1, r]).astype(BF16)
        rows = jnp.dot(vct[:, lo:hi], k, preferred_element_type=F32)
        orr[:, r] = rows if first_rows else orr[:, r] + rows
        n = hi - lo
        pt[:, 0:n] = k.T
        cols = jnp.dot(vrt[:, r], pt[:, 0:n], preferred_element_type=F32)
        oc[:, lo:hi] = cols if first_cols else oc[:, lo:hi] + cols

    row_out, col_out = ([], [])

    def send_rows(p):
        rt = orr[:, 512 * p : 512 * p + 512].T.astype(BF16)
        for j in range(8):
            n = 8 * p + j
            rsend[n] = jnp.concatenate(
                [rt[64 * j : 64 * j + 32], rt[64 * j + 32 : 64 * j + 64]], axis=1
            )
        for j in range(8):
            n = 8 * p + j
            dz, dy = (Z_OFF[n // 4], Y_OFF[n % 4])
            if (dz, dy) != (0, 0):
                row_out.append(
                    send(rsend.at[n], rrecv.at[n], rr_s.at[n], rr_r.at[n], dev(dy=dy, dz=dz))
                )

    def send_cols(*slots):
        for n in slots:
            at = slice(512 * n, 512 * n + 512)
            csend[:, at] = oc[:, at].astype(BF16)
        for n in slots:
            at = slice(512 * n, 512 * n + 512)
            if n:
                to = dev(dx=X_OFF[n % 4], other=n // 4)
                col_out.append(send(csend.at[:, at], crecv.at[n], cc_s.at[n], cc_r.at[n], to))

    partner = embed_cols(0)
    arrive(ys)
    z1 = z_step(1)
    embed_rows(7)
    xs[2, 0].wait_recv()
    xs[3, 0] = send(half(2, 0), half(3, 0), x_s.at[6], x_r.at[6], dev(dx=1))
    xs[1, 1].wait_recv()
    xs[3, 1] = send(half(1, 1), half(3, 1), x_s.at[7], x_r.at[7], dev(dx=-1))
    arrive([xs[2, 1], xs[1, 0]])
    partner += embed_cols(1, 2)
    arrive(z1)
    z2 = z_step(2)
    embed_rows(6, 5)
    arrive([xs[3, 0], xs[3, 1]])
    partner += embed_cols(3)
    arrive(z2)
    z3 = z_step(3)
    embed_rows(4, 1)
    panel(3, 0, 2048, True, True)
    arrive(z3)
    z4 = z_step(4)
    embed_rows(0, 3)
    panel(2, 0, 2048, True, False)
    panel(0, 0, 2048, True, False)
    arrive(z4)
    embed_rows(2)
    panel(1, 0, 2048, True, False)
    send_cols(3, 2, 1, 0)
    arrive(partner)
    for s in range(4, 8):
        at = slice(512 * s, 512 * s + 512)
        cn[at, :] = jnp.broadcast_to(half_sq(fc[at, :]), (512, 128))
    panel(1, 2048, 4096, False, True)
    send_rows(1)
    panel(0, 2048, 4096, False, False)
    send_rows(0)
    panel(2, 3072, 4096, False, False)
    panel(3, 3072, 4096, False, False)
    send_cols(7, 6)
    panel(2, 2048, 3072, False, False)
    send_rows(2)
    panel(3, 2048, 3072, False, False)
    send_cols(5, 4)
    send_rows(3)

    scale = sig[0]
    arrive(row_out)
    total = rsend[28].astype(F32)
    for n in range(32):
        if n != 28:
            total += rrecv[n].astype(F32)
    total = total * scale
    rout[0:32, :] = total[:, 0:64]
    rout[32:64, :] = total[:, 64:128]
    arrive(col_out)
    total = csend[:, 0:512].astype(F32)
    for n in range(1, 8):
        total += crecv[n].astype(F32)
    cout[...] = total * scale
    for c in sent:
        c.wait_send()


def body(rp, cp, rv, cv, w1, b1, w2, b2, w3, ard, sig):
    vmem = pl.BlockSpec(memory_space=pltpu.VMEM)
    away = pl.BlockSpec(memory_space=pl.ANY)
    dma = pltpu.SemaphoreType.DMA
    rows, cols = pl.pallas_call(
        kernel,
        out_shape=(jax.ShapeDtypeStruct((64, 64), F32), jax.ShapeDtypeStruct((64, 512), F32)),
        in_specs=[away] * 5 + [vmem, away, vmem, away, vmem, pl.BlockSpec(memory_space=pltpu.SMEM)],
        out_specs=(vmem, vmem),
        scratch_shapes=[
            pltpu.VMEM((128, 512), BF16),
            pltpu.VMEM((512, 512), BF16),
            pltpu.VMEM((512, 256), BF16),
            pltpu.VMEM((64, 64), BF16),
            pltpu.VMEM((64, 64), BF16),
            pltpu.VMEM((2048, 128), BF16),
            pltpu.VMEM((4, 128, 512), BF16),
            pltpu.VMEM((2048, 256), BF16),
            pltpu.VMEM((4096, 256), BF16),
            pltpu.VMEM((64, 2048), BF16),
            pltpu.VMEM((64, 4096), BF16),
            pltpu.VMEM((8, 2048), F32),
            pltpu.VMEM((4096, 128), F32),
            pltpu.VMEM((512, 2048), BF16),
            pltpu.VMEM((64, 4096), F32),
            pltpu.VMEM((64, 2048), F32),
            pltpu.VMEM((32, 32, 128), BF16),
            pltpu.VMEM((32, 32, 128), BF16),
            pltpu.VMEM((64, 4096), BF16),
            pltpu.VMEM((8, 64, 512), BF16),
            dma((7,)), dma((4,)), dma((4,)), dma((8,)), dma((8,)), dma((8,)), dma((8,)),
            dma((8,)), dma((8,)), dma((32,)), dma((32,)), dma((8,)), dma((8,)),
        ],
        compiler_params=pltpu.CompilerParams(
            collective_id=0, has_side_effects=True, vmem_limit_bytes=62 * 2**20
        ),
    )(
        rp, rv, cp.T, cv.T, w1, b1.reshape(1, -1), w2, b2.reshape(1, -1), w3,
        ard.reshape(1, -1), sig,
    )
    return (rows, cols.T)


def solution(mesh):
    rows, cols = (P(("row", "col"), None), P(("col", "row"), None))
    in_specs = (rows, cols, rows, cols) + (P(),) * 7
    return jax.shard_map(
        body, mesh=mesh, in_specs=in_specs, out_specs=(rows, cols), check_vma=False
    )
```

time: 68.9 us -> 50.4 us (0.73)
  Pallas kernels: 62.7 us -> 45.9 us
  local copies, waits for them, and re-layouts: 4.76 us -> 2.94 us
    pallas_call x1, Pallas kernels: 62.7 us -> 45.9 us  [body(): pl.pallas_call(kernel, out_shape=(jax.ShapeDtypeStruct((64, 64), F32), ja...]
    pallas_call x1 -> x0, local copies, waits for them, and re-layouts: 1.73 us -> none  [body(): pl.pallas_call(kernel, out_shape=(jax.ShapeDtypeStruct((64, 64), F32), ja...]
    unnamed x7 -> x2, local copies, waits for them, and re-layouts: 3.03 us -> 2.94 us
where the time goes in v2:
time: 50.4 us; the launch traced here: 50.1 us
  Pallas kernels  45.9 us (91%)
  local copies, waits for them, and re-layouts  2.94 us (6%)
  between operations  1.29 us (3%)
    pallas_call x1, Pallas kernels, body(): pl.pallas_call(kernel, out_shape=(jax.ShapeDtypeStruct((64, 64), F32), ja...  45.9 us
    unnamed x2, local copies, waits for them, and re-layouts  2.94 us

profile of v2, /device:TPU:1, one launch (start us, length us, event | category | flops | bytes accessed | tf_op | source)
XLA Modules:
  0.0 50.1 jit_solution(12649604354120962452)
XLA Ops:
  1.3 45.9 %shard_map.122 = (f32[64,64]{1,0:T(8,128)}, f32[64,512]{1,0:T(8,128)}) custom-call(bf16[64,64]{1,0:T(8,128)(2,1)} %rp.1, bf16[64,64]{1,0:T(8,128)(2,1)} %rv.1, bf16[64,512]{1,0:T(8,128)(2,1)} %bitcast.7, bf16[64,512]{1,0:T(8,128)(2,1)} %bitcast.8, bf16[64,512]{1,0:T(8,128)(2,1)} %w1.1, f32[1,512]{1,0:T(1,128)} %bitcast.9, bf16[512,512]{1,0:T(8,128)(2,1)} %w2.1, ...), custom_call_target="tpu_custom_call" | custom-call | tf_op jit(solution)/shard_map/pallas_call | solution.py:258
  47.2 1.4 %copy.16 = f32[64,64]{1,0:T(8,128)} copy(f32[64,64]{1,0:T(8,128)} %get-tuple-element.8) | data formatting | bytes 32768
  48.6 1.6 %copy.17 = f32[512,64]{0,1:T(8,128)} copy(f32[512,64]{0,1:T(8,128)} %bitcast.6) | data formatting | bytes 262144

commit v3 on v2

--- a/solution.py
+++ b/solution.py
@@ -11,15 +11,14 @@
 LOG2E = 1.4426950408889634
 
 NX, NY, NZ = (4, 4, 8)
-Z_OFF = (-3, 2, 4, 3, -2, 1, -1, 0)
+Z_OFF = (0, -1, 1, -2, 2, -3, 3, 4)
 Y_OFF = (0, -1, 1, 2)
 X_OFF = (0, 1, -1, 2)
-MINUS = {0: 7, 1: 6, 2: 4, 3: 0, 4: 2}
-PLUS = {0: 7, 1: 5, 2: 1, 3: 3}
+BATCHES = ((0, 3), (3, 5), (5, 8))
 
 
 def kernel(
-    rp, rv, cp, cv, w1, b1, w2, b2, w3, ard, sig,
+    rp, rv, cp, cv, w1, b1, w2, b2, w3, ard,
     rout, cout,
     w1v, w2v, w3v, rpv, rvv, xr, xc, rf, fc, vrt, vct, rn, cn, pt, oc, orr,
     rsend, rrecv, csend, crecv,
@@ -48,8 +47,8 @@
         sent.append(c)
         return c
 
-    peers = [dict(other=1)] + [dict(dx=d) for d in (1, -1)]
-    peers += [dict(dy=d) for d in (1, -1, 2)] + [dict(dz=d) for d in (1, -1)]
+    peers = [dict(other=1)] + [dict(dx=d) for d in X_OFF[1:]]
+    peers += [dict(dy=d) for d in Y_OFF[1:]] + [dict(dz=d) for d in Z_OFF[1:]]
     barrier = pltpu.get_barrier_semaphore()
     for q in peers:
         pl.semaphore_signal(barrier, inc=1, device_id=dev(**q), device_id_type=MESH)
@@ -65,30 +64,8 @@
     w1v[64:128, :] = jnp.zeros((64, 512), BF16)
     local[0].wait()
     local[1].wait()
-    xr[1792:1856, :] = jnp.concatenate([rpv[...], rvv[...]], axis=1)
-    local[2].wait()
-    local[3].wait()
-    pl.semaphore_wait(barrier, len(peers))
-
-    ys = []
-    for j, dy in enumerate(Y_OFF):
-        if j:
-            ys.append(
-                send(
-                    xr.at[1792:1856], xr.at[1792 + 64 * j : 1856 + 64 * j],
-                    y_s.at[j], y_r.at[j], dev(dy=-dy),
-                )
-            )
-
-    def half(slot, h):
-        return xc.at[slot, :, 256 * h : 256 * h + 256]
-
-    xs = {}
-    for h in (0, 1):
-        xs[2, h] = send(half(0, h), half(2, h), x_s.at[4 + h], x_r.at[4 + h], dev(dx=1))
-        g = 1 - h
-        xs[1, g] = send(half(0, g), half(1, g), x_s.at[2 + g], x_r.at[2 + g], dev(dx=-1))
-    for c in local[4:]:
+    xr[0:64, :] = jnp.concatenate([rpv[...], rvv[...]], axis=1)
+    for c in local[2:]:
         c.wait()
 
     def embed(pre):
@@ -112,6 +89,8 @@
             fc[512 * s : 512 * s + 512, :] = part
             cn[512 * s : 512 * s + 512, :] = jnp.broadcast_to(half_sq(part), (512, 128))
             vct[:, 512 * s : 512 * s + 512] = xc[s, 64:128, :]
+
+    def share_cols(*slots):
         done = []
         for s in slots:
             lo, hi = (slice(512 * s, 512 * s + 512), slice(2048 + 512 * s, 2560 + 512 * s))
@@ -121,27 +100,13 @@
             )
         return done
 
-    def embed_rows(*slots):
-        raw = jnp.concatenate([xr[256 * s : 256 * s + 256, :] for s in slots], axis=0)
+    def embed_rows(p):
+        at = slice(512 * p, 512 * p + 512)
+        raw = xr[at, :]
         feats = embed(jnp.dot(raw, w1v[...], preferred_element_type=F32))
-        values = raw.T
-        norms = jnp.broadcast_to(half_sq(feats), (256 * len(slots), 128)).T
-        for i, s in enumerate(slots):
-            here, there = (slice(256 * i, 256 * i + 256), slice(256 * s, 256 * s + 256))
-            rf[there, :] = feats[here]
-            vrt[:, there] = values[64:128, here]
-            rn[:, there] = norms[0:8, here]
-
-    def z_step(step):
-        now = []
-        for table, d in ((MINUS, 1), (PLUS, -1)):
-            if step in table:
-                a, b = (table[step - 1] * 256, table[step] * 256)
-                i = table[step]
-                now.append(
-                    send(xr.at[a : a + 256], xr.at[b : b + 256], z_s.at[i], z_r.at[i], dev(dz=d))
-                )
-        return now
+        rf[at, :] = feats
+        vrt[:, at] = raw.T[64:128, :]
+        rn[:, at] = jnp.broadcast_to(half_sq(feats), (512, 128)).T[0:8, :]
 
     def arrive(copies):
         for c in copies:
@@ -159,7 +124,14 @@
         n = hi - lo
         pt[:, 0:n] = k.T
         cols = jnp.dot(vrt[:, r], pt[:, 0:n], preferred_element_type=F32)
-        oc[:, lo:hi] = cols if first_cols else oc[:, lo:hi] + cols
+        if first_cols is True:
+            oc[:, lo:hi] = cols
+        elif first_cols:
+            m = first_cols[1]
+            oc[:, lo:m] += cols[:, 0 : m - lo]
+            oc[:, m:hi] = cols[:, m - lo :]
+        else:
+            oc[:, lo:hi] += cols
 
     row_out, col_out = ([], [])
 
@@ -172,7 +144,7 @@
             )
         for j in range(8):
             n = 8 * p + j
-            dz, dy = (Z_OFF[n // 4], Y_OFF[n % 4])
+            dz, dy = (Z_OFF[n % 8], Y_OFF[n // 8])
             if (dz, dy) != (0, 0):
                 row_out.append(
                     send(rsend.at[n], rrecv.at[n], rr_s.at[n], rr_r.at[n], dev(dy=dy, dz=dz))
@@ -188,67 +160,81 @@
                 to = dev(dx=X_OFF[n % 4], other=n // 4)
                 col_out.append(send(csend.at[:, at], crecv.at[n], cc_s.at[n], cc_r.at[n], to))
 
-    partner = embed_cols(0)
-    arrive(ys)
-    z1 = z_step(1)
-    embed_rows(7)
-    xs[2, 0].wait_recv()
-    xs[3, 0] = send(half(2, 0), half(3, 0), x_s.at[6], x_r.at[6], dev(dx=1))
-    xs[1, 1].wait_recv()
-    xs[3, 1] = send(half(1, 1), half(3, 1), x_s.at[7], x_r.at[7], dev(dx=-1))
-    arrive([xs[2, 1], xs[1, 0]])
-    partner += embed_cols(1, 2)
-    arrive(z1)
-    z2 = z_step(2)
-    embed_rows(6, 5)
-    arrive([xs[3, 0], xs[3, 1]])
-    partner += embed_cols(3)
-    arrive(z2)
-    z3 = z_step(3)
-    embed_rows(4, 1)
-    panel(3, 0, 2048, True, True)
-    arrive(z3)
-    z4 = z_step(4)
-    embed_rows(0, 3)
+    embed_cols(0)
+    pl.semaphore_wait(barrier, len(peers))
+    zs = []
+    for i, d in enumerate(Z_OFF):
+        if i:
+            zs.append(
+                send(xr.at[0:64], xr.at[64 * i : 64 * i + 64], z_s.at[i], z_r.at[i], dev(dz=-d))
+            )
+    xs = [None]
+    for j, d in enumerate(X_OFF):
+        if j:
+            xs.append(send(xc.at[0], xc.at[j], x_s.at[j], x_r.at[j], dev(dx=-d)))
+    partner = share_cols(0)
+    ys = {1: [], 2: [], 3: []}
+    for n, (lo, hi) in enumerate(BATCHES):
+        arrive(zs[max(lo, 1) - 1 : hi - 1])
+        for j, d in enumerate(Y_OFF):
+            if j:
+                i = 3 * j + n
+                a, b = (slice(64 * lo, 64 * hi), slice(512 * j + 64 * lo, 512 * j + 64 * hi))
+                ys[j].append(send(xr.at[a], xr.at[b], y_s.at[i], y_r.at[i], dev(dy=-d)))
+    embed_rows(0)
+    arrive(xs[1:3])
+    embed_cols(1, 2)
+    partner += share_cols(1, 2)
+    panel(0, 0, 1536, True, True)
+    arrive(xs[3:])
+    embed_cols(3)
+    partner += share_cols(3)
+    arrive(ys[1])
+    embed_rows(1)
+    panel(1, 0, 2048, True, (0, 1536))
+    arrive(ys[2])
+    embed_rows(2)
     panel(2, 0, 2048, True, False)
-    panel(0, 0, 2048, True, False)
-    arrive(z4)
-    embed_rows(2)
-    panel(1, 0, 2048, True, False)
+    arrive(ys[3])
+    embed_rows(3)
+    panel(3, 0, 2048, True, False)
+    panel(0, 1536, 2048, False, False)
     send_cols(3, 2, 1, 0)
     arrive(partner)
     for s in range(4, 8):
         at = slice(512 * s, 512 * s + 512)
         cn[at, :] = jnp.broadcast_to(half_sq(fc[at, :]), (512, 128))
-    panel(1, 2048, 4096, False, True)
+    panel(3, 2048, 4096, False, True)
+    send_rows(3)
+    panel(2, 2048, 4096, False, False)
+    send_rows(2)
+    panel(1, 3072, 4096, False, False)
+    panel(0, 3072, 4096, False, False)
+    send_cols(7, 6)
+    panel(1, 2048, 3072, False, False)
     send_rows(1)
-    panel(0, 2048, 4096, False, False)
+    panel(0, 2048, 3072, False, False)
+    send_cols(5, 4)
     send_rows(0)
-    panel(2, 3072, 4096, False, False)
-    panel(3, 3072, 4096, False, False)
-    send_cols(7, 6)
-    panel(2, 2048, 3072, False, False)
-    send_rows(2)
-    panel(3, 2048, 3072, False, False)
-    send_cols(5, 4)
-    send_rows(3)
-
-    scale = sig[0]
+
     arrive(row_out)
-    total = rsend[28].astype(F32)
-    for n in range(32):
-        if n != 28:
-            total += rrecv[n].astype(F32)
-    total = total * scale
+    total = rsend[0].astype(F32)
+    for n in range(1, 32):
+        total += rrecv[n].astype(F32)
     rout[0:32, :] = total[:, 0:64]
     rout[32:64, :] = total[:, 64:128]
     arrive(col_out)
     total = csend[:, 0:512].astype(F32)
     for n in range(1, 8):
         total += crecv[n].astype(F32)
-    cout[...] = total * scale
+    cout[...] = total
     for c in sent:
         c.wait_send()
+
+
+def finish(rin, cin, sig, rout, cout):
+    rout[...] = rin[...] * sig[0]
+    cout[...] = cin[...] * sig[0]
 
 
 def body(rp, cp, rv, cv, w1, b1, w2, b2, w3, ard, sig):
@@ -258,7 +244,7 @@
     rows, cols = pl.pallas_call(
         kernel,
         out_shape=(jax.ShapeDtypeStruct((64, 64), F32), jax.ShapeDtypeStruct((64, 512), F32)),
-        in_specs=[away] * 5 + [vmem, away, vmem, away, vmem, pl.BlockSpec(memory_space=pltpu.SMEM)],
+        in_specs=[away] * 5 + [vmem, away, vmem, away, vmem],
         out_specs=(vmem, vmem),
         scratch_shapes=[
             pltpu.VMEM((128, 512), BF16),
@@ -281,7 +267,7 @@
             pltpu.VMEM((32, 32, 128), BF16),
             pltpu.VMEM((64, 4096), BF16),
             pltpu.VMEM((8, 64, 512), BF16),
-            dma((7,)), dma((4,)), dma((4,)), dma((8,)), dma((8,)), dma((8,)), dma((8,)),
+            dma((7,)), dma((12,)), dma((12,)), dma((8,)), dma((8,)), dma((4,)), dma((4,)),
             dma((8,)), dma((8,)), dma((32,)), dma((32,)), dma((8,)), dma((8,)),
         ],
         compiler_params=pltpu.CompilerParams(
@@ -289,8 +275,14 @@
         ),
     )(
         rp, rv, cp.T, cv.T, w1, b1.reshape(1, -1), w2, b2.reshape(1, -1), w3,
-        ard.reshape(1, -1), sig,
+        ard.reshape(1, -1),
     )
+    rows, cols = pl.pallas_call(
+        finish,
+        out_shape=(jax.ShapeDtypeStruct((64, 64), F32), jax.ShapeDtypeStruct((64, 512), F32)),
+        in_specs=[vmem, vmem, pl.BlockSpec(memory_space=pltpu.SMEM)],
+        out_specs=(vmem, vmem),
+    )(rows, cols, sig)
     return (rows, cols.T)
 
 

time: 50.4 us -> 46.6 us (0.925)
  local copies, waits for them, and re-layouts: 2.94 us -> 0 us
  Pallas kernels: 45.9 us -> 45.1 us
    unnamed x2 -> x0, local copies, waits for them, and re-layouts: 2.94 us -> none
    pallas_call x1, Pallas kernels: 45.9 us -> 43.5 us  [body(): pl.pallas_call(kernel, out_shape=(jax.ShapeDtypeStruct((64, 64), F32), ja...]
    pallas_call x0 -> x1, Pallas kernels: none -> 1.6 us  [body(): pl.pallas_call(finish, out_shape=(jax.ShapeDtypeStruct((64, 64), F32), ja...]
where the time goes in v3:
time: 46.6 us; the launch traced here: 46.4 us
  Pallas kernels  45.1 us (97%)
  between operations  1.29 us (3%)
    pallas_call x1, Pallas kernels, body(): pl.pallas_call(kernel, out_shape=(jax.ShapeDtypeStruct((64, 64), F32), ja...  43.5 us
    pallas_call x1, Pallas kernels, body(): pl.pallas_call(finish, out_shape=(jax.ShapeDtypeStruct((64, 64), F32), ja...  1.6 us

profile of v3, /device:TPU:1, one launch (start us, length us, event | category | flops | bytes accessed | tf_op | source)
XLA Modules:
  0.0 46.4 jit_solution(16429818013635776538)
XLA Ops:
  1.3 43.5 %shard_map.122 = (f32[64,64]{1,0:T(8,128)}, f32[64,512]{1,0:T(8,128)}) custom-call(bf16[64,64]{1,0:T(8,128)(2,1)} %rp.1, bf16[64,64]{1,0:T(8,128)(2,1)} %rv.1, bf16[64,512]{1,0:T(8,128)(2,1)} %bitcast.6, bf16[64,512]{1,0:T(8,128)(2,1)} %bitcast.7, bf16[64,512]{1,0:T(8,128)(2,1)} %w1.1, f32[1,512]{1,0:T(1,128)} %bitcast.8, bf16[512,512]{1,0:T(8,128)(2,1)} %w2.1, ...), custom_call_target="tpu_custom_call" | custom-call | tf_op jit(solution)/shard_map/pallas_call | solution.py:244
  44.8 1.6 %shard_map.123 = (f32[64,64]{1,0:T(8,128)}, f32[64,512]{1,0:T(8,128)}) custom-call(f32[64,64]{1,0:T(8,128)} %get-tuple-element.6.rin, f32[64,512]{1,0:T(8,128)} %get-tuple-element.7.cin, f32[1]{0:T(128)S(6)} %copy.13.sig), custom_call_target="tpu_custom_call" | custom-call | tf_op jit(solution)/shard_map/pallas_call | solution.py:280

commit v4 on v3

--- a/solution.py
+++ b/solution.py
@@ -14,13 +14,14 @@
 Z_OFF = (0, -1, 1, -2, 2, -3, 3, 4)
 Y_OFF = (0, -1, 1, 2)
 X_OFF = (0, 1, -1, 2)
+BLOCKS = tuple((i, 0) for i in range(8)) + tuple((i, j) for i in range(8) for j in (1, 2, 3))
 BATCHES = ((0, 3), (3, 5), (5, 8))
 
 
 def kernel(
-    rp, rv, cp, cv, w1, b1, w2, b2, w3, ard,
+    rp, rv, cp, cv, w1, b1h, w2, b2h, w3, ardh,
     rout, cout,
-    w1v, w2v, w3v, rpv, rvv, xr, xc, rf, fc, vrt, vct, rn, cn, pt, oc, orr,
+    w1v, w2v, w3v, b1, b2, ard, rpv, rvv, xr, xo, xc, rf, fc, vrt, vct, rn, cn, pt, oc, orr,
     rsend, rrecv, csend, crecv,
     l_s, y_s, y_r, z_s, z_r, x_s, x_r, p_s, p_r, rr_s, rr_r, cc_s, cc_r,
 ):
@@ -56,7 +57,7 @@
     local = []
     for i, (a, b) in enumerate(
         ((rp, rpv), (rv, rvv), (cp, xc.at[0, 0:64]), (cv, xc.at[0, 64:128]), (w1, w1v.at[0:64]),
-         (w2, w2v), (w3, w3v))
+         (w2, w2v), (w3, w3v), (b1h, b1), (b2h, b2), (ardh, ard))
     ):
         c = pltpu.make_async_copy(a, b, l_s.at[i])
         c.start()
@@ -64,8 +65,8 @@
     w1v[64:128, :] = jnp.zeros((64, 512), BF16)
     local[0].wait()
     local[1].wait()
-    xr[0:64, :] = jnp.concatenate([rpv[...], rvv[...]], axis=1)
-    for c in local[2:]:
+    xr[0] = jnp.concatenate([rpv[...], rvv[...]], axis=1)
+    for c in local[2:4]:
         c.wait()
 
     def embed(pre):
@@ -78,17 +79,18 @@
         f = feats.astype(F32)
         return (-0.5 * LOG2E) * jnp.sum(f * f, axis=1, keepdims=True)
 
-    def embed_cols(*slots):
-        points = jnp.concatenate([xc[s, 0:64, :] for s in slots], axis=1)
+    def embed_cols(n, *starts):
+        blocks = [(at // 512, slice(at % 512, at % 512 + n)) for at in starts]
+        points = jnp.concatenate([xc[j, 0:64, lanes] for j, lanes in blocks], axis=1)
         pre = lax.dot_general(
             points, w1v[0:64, :], (((0,), (0,)), ((), ())), preferred_element_type=F32
         )
         feats = embed(pre)
-        for i, s in enumerate(slots):
-            part = feats[512 * i : 512 * i + 512]
-            fc[512 * s : 512 * s + 512, :] = part
-            cn[512 * s : 512 * s + 512, :] = jnp.broadcast_to(half_sq(part), (512, 128))
-            vct[:, 512 * s : 512 * s + 512] = xc[s, 64:128, :]
+        for i, (at, (j, lanes)) in enumerate(zip(starts, blocks)):
+            part = feats[n * i : n * i + n]
+            fc[at : at + n, :] = part
+            cn[at : at + n, :] = jnp.broadcast_to(half_sq(part), (n, 128))
+            vct[:, at : at + n] = xc[j, 64:128, lanes]
 
     def share_cols(*slots):
         done = []
@@ -98,11 +100,13 @@
             done.append(
                 send(vct.at[:, lo], vct.at[:, hi], p_s.at[4 + s], p_r.at[4 + s], dev(other=1))
             )
+            done.append(send(cn.at[lo], cn.at[hi], p_s.at[8 + s], p_r.at[8 + s], dev(other=1)))
         return done
 
     def embed_rows(p):
         at = slice(512 * p, 512 * p + 512)
-        raw = xr[at, :]
+        blocks = BLOCKS[8 * p : 8 * p + 8]
+        raw = jnp.concatenate([xo[i, j - 1] if j else xr[i] for i, j in blocks], axis=0)
         feats = embed(jnp.dot(raw, w1v[...], preferred_element_type=F32))
         rf[at, :] = feats
         vrt[:, at] = raw.T[64:128, :]
@@ -112,7 +116,11 @@
         for c in copies:
             c.wait_recv()
 
-    def panel(p, lo, hi, first_rows, first_cols):
+    turn = [0]
+
+    def panel(p, lo, hi):
+        first_rows, first_cols = (lo == 0, p == 0)
+        turn[0] = 1 - turn[0]
         r = slice(512 * p, 512 * p + 512)
         inner = lax.dot_general(
             fc[lo:hi, :], rf[r, :], (((1,), (1,)), ((), ())), preferred_element_type=F32
@@ -122,16 +130,10 @@
         rows = jnp.dot(vct[:, lo:hi], k, preferred_element_type=F32)
         orr[:, r] = rows if first_rows else orr[:, r] + rows
         n = hi - lo
-        pt[:, 0:n] = k.T
-        cols = jnp.dot(vrt[:, r], pt[:, 0:n], preferred_element_type=F32)
-        if first_cols is True:
-            oc[:, lo:hi] = cols
-        elif first_cols:
-            m = first_cols[1]
-            oc[:, lo:m] += cols[:, 0 : m - lo]
-            oc[:, m:hi] = cols[:, m - lo :]
-        else:
-            oc[:, lo:hi] += cols
+        flip = pt.at[turn[0], :, 0:n]
+        flip[...] = k.T
+        cols = jnp.dot(vrt[:, r], flip[...], preferred_element_type=F32)
+        oc[:, lo:hi] = cols if first_cols else oc[:, lo:hi] + cols
 
     row_out, col_out = ([], [])
 
@@ -144,7 +146,7 @@
             )
         for j in range(8):
             n = 8 * p + j
-            dz, dy = (Z_OFF[n % 8], Y_OFF[n // 8])
+            dz, dy = (Z_OFF[BLOCKS[n][0]], Y_OFF[BLOCKS[n][1]])
             if (dz, dy) != (0, 0):
                 row_out.append(
                     send(rsend.at[n], rrecv.at[n], rr_s.at[n], rr_r.at[n], dev(dy=dy, dz=dz))
@@ -160,62 +162,75 @@
                 to = dev(dx=X_OFF[n % 4], other=n // 4)
                 col_out.append(send(csend.at[:, at], crecv.at[n], cc_s.at[n], cc_r.at[n], to))
 
-    embed_cols(0)
     pl.semaphore_wait(barrier, len(peers))
     zs = []
     for i, d in enumerate(Z_OFF):
         if i:
             zs.append(
-                send(xr.at[0:64], xr.at[64 * i : 64 * i + 64], z_s.at[i], z_r.at[i], dev(dz=-d))
+                send(xr.at[0], xr.at[i], z_s.at[i], z_r.at[i], dev(dz=-d))
             )
-    xs = [None]
-    for j, d in enumerate(X_OFF):
-        if j:
-            xs.append(send(xc.at[0], xc.at[j], x_s.at[j], x_r.at[j], dev(dx=-d)))
+    xs = {}
+    for h in (0, 1):
+        for j in (1, 2):
+            part = (slice(None), slice(256 * h, 256 * h + 256))
+            i = 2 * j + h
+            xs[j, h] = send(
+                xc.at[0].at[part], xc.at[j].at[part], x_s.at[i], x_r.at[i], dev(dx=-X_OFF[j])
+            )
+    xs[3] = send(xc.at[0], xc.at[3], x_s.at[0], x_r.at[0], dev(dx=-X_OFF[3]))
+    for c in local[4:]:
+        c.wait()
+    embed_cols(512, 0)
     partner = share_cols(0)
-    ys = {1: [], 2: [], 3: []}
-    for n, (lo, hi) in enumerate(BATCHES):
+    ys = []
+
+    def relay(n):
+        lo, hi = BATCHES[n]
         arrive(zs[max(lo, 1) - 1 : hi - 1])
         for j, d in enumerate(Y_OFF):
             if j:
                 i = 3 * j + n
-                a, b = (slice(64 * lo, 64 * hi), slice(512 * j + 64 * lo, 512 * j + 64 * hi))
-                ys[j].append(send(xr.at[a], xr.at[b], y_s.at[i], y_r.at[i], dev(dy=-d)))
+                a, b = (xr.at[lo:hi], xo.at[lo:hi, j - 1])
+                ys.append(send(a, b, y_s.at[i], y_r.at[i], dev(dy=-d)))
+
+    relay(0)
+    arrive([xs[1, 0], xs[2, 0]])
+    embed_cols(256, 512, 1024)
+    relay(1)
+    arrive([xs[1, 1], xs[2, 1]])
+    embed_cols(256, 768, 1280)
+    partner += share_cols(1, 2)
+    relay(2)
     embed_rows(0)
-    arrive(xs[1:3])
-    embed_cols(1, 2)
-    partner += share_cols(1, 2)
-    panel(0, 0, 1536, True, True)
-    arrive(xs[3:])
-    embed_cols(3)
-    partner += share_cols(3)
-    arrive(ys[1])
+    panel(0, 0, 1536)
+    arrive([xs[3]])
+    embed_cols(512, 1536)
+    last = share_cols(3)
+    arrive(partner)
+    panel(0, 1536, 2048)
+    panel(0, 2048, 3584)
+    arrive(last)
+    arrive(ys)
+    panel(0, 3584, 4096)
+    embed_rows(3)
+    embed_rows(2)
     embed_rows(1)
-    panel(1, 0, 2048, True, (0, 1536))
-    arrive(ys[2])
-    embed_rows(2)
-    panel(2, 0, 2048, True, False)
-    arrive(ys[3])
-    embed_rows(3)
-    panel(3, 0, 2048, True, False)
-    panel(0, 1536, 2048, False, False)
+    send_rows(0)
+    panel(3, 0, 2048)
+    panel(3, 2048, 4096)
+    send_rows(3)
+    panel(2, 0, 2048)
+    panel(1, 0, 2048)
     send_cols(3, 2, 1, 0)
-    arrive(partner)
-    for s in range(4, 8):
-        at = slice(512 * s, 512 * s + 512)
-        cn[at, :] = jnp.broadcast_to(half_sq(fc[at, :]), (512, 128))
-    panel(3, 2048, 4096, False, True)
-    send_rows(3)
-    panel(2, 2048, 4096, False, False)
+    panel(2, 2048, 4096)
+    panel(1, 3072, 4096)
     send_rows(2)
-    panel(1, 3072, 4096, False, False)
-    panel(0, 3072, 4096, False, False)
     send_cols(7, 6)
-    panel(1, 2048, 3072, False, False)
+    panel(1, 2560, 3072)
+    send_cols(5)
+    panel(1, 2048, 2560)
     send_rows(1)
-    panel(0, 2048, 3072, False, False)
-    send_cols(5, 4)
-    send_rows(0)
+    send_cols(4)
 
     arrive(row_out)
     total = rsend[0].astype(F32)
@@ -244,15 +259,19 @@
     rows, cols = pl.pallas_call(
         kernel,
         out_shape=(jax.ShapeDtypeStruct((64, 64), F32), jax.ShapeDtypeStruct((64, 512), F32)),
-        in_specs=[away] * 5 + [vmem, away, vmem, away, vmem],
+        in_specs=[away] * 10,
         out_specs=(vmem, vmem),
         scratch_shapes=[
             pltpu.VMEM((128, 512), BF16),
             pltpu.VMEM((512, 512), BF16),
             pltpu.VMEM((512, 256), BF16),
+            pltpu.VMEM((1, 512), F32),
+            pltpu.VMEM((1, 512), F32),
+            pltpu.VMEM((1, 256), F32),
             pltpu.VMEM((64, 64), BF16),
             pltpu.VMEM((64, 64), BF16),
-            pltpu.VMEM((2048, 128), BF16),
+            pltpu.VMEM((8, 64, 128), BF16),
+            pltpu.VMEM((8, 3, 64, 128), BF16),
             pltpu.VMEM((4, 128, 512), BF16),
             pltpu.VMEM((2048, 256), BF16),
             pltpu.VMEM((4096, 256), BF16),
@@ -260,15 +279,15 @@
             pltpu.VMEM((64, 4096), BF16),
             pltpu.VMEM((8, 2048), F32),
             pltpu.VMEM((4096, 128), F32),
-            pltpu.VMEM((512, 2048), BF16),
+            pltpu.VMEM((2, 512, 2048), BF16),
             pltpu.VMEM((64, 4096), F32),
             pltpu.VMEM((64, 2048), F32),
             pltpu.VMEM((32, 32, 128), BF16),
             pltpu.VMEM((32, 32, 128), BF16),
             pltpu.VMEM((64, 4096), BF16),
             pltpu.VMEM((8, 64, 512), BF16),
-            dma((7,)), dma((12,)), dma((12,)), dma((8,)), dma((8,)), dma((4,)), dma((4,)),
-            dma((8,)), dma((8,)), dma((32,)), dma((32,)), dma((8,)), dma((8,)),
+            dma((10,)), dma((12,)), dma((12,)), dma((8,)), dma((8,)), dma((8,)), dma((8,)),
+            dma((12,)), dma((12,)), dma((32,)), dma((32,)), dma((8,)), dma((8,)),
         ],
         compiler_params=pltpu.CompilerParams(
             collective_id=0, has_side_effects=True, vmem_limit_bytes=62 * 2**20

time: 46.6 us -> 44.2 us (0.948)
  Pallas kernels: 45.1 us -> 42.7 us
    pallas_call x1, Pallas kernels: 43.5 us -> 41.1 us  [body(): pl.pallas_call(kernel, out_shape=(jax.ShapeDtypeStruct((64, 64), F32), ja...]
where the time goes in v4:
time: 44.2 us; the launch traced here: 44 us
  Pallas kernels  42.7 us (97%)
  between operations  1.29 us (3%)
    pallas_call x1, Pallas kernels, body(): pl.pallas_call(kernel, out_shape=(jax.ShapeDtypeStruct((64, 64), F32), ja...  41.1 us
    pallas_call x1, Pallas kernels, body(): pl.pallas_call(finish, out_shape=(jax.ShapeDtypeStruct((64, 64), F32), ja...  1.6 us

profile of v4, /device:TPU:1, one launch (start us, length us, event | category | flops | bytes accessed | tf_op | source)
XLA Modules:
  0.0 44.0 jit_solution(7344533416161329396)
XLA Ops:
  1.3 41.1 %shard_map.122 = (f32[64,64]{1,0:T(8,128)}, f32[64,512]{1,0:T(8,128)}) custom-call(bf16[64,64]{1,0:T(8,128)(2,1)} %rp.1, bf16[64,64]{1,0:T(8,128)(2,1)} %rv.1, bf16[64,512]{1,0:T(8,128)(2,1)} %bitcast.6, bf16[64,512]{1,0:T(8,128)(2,1)} %bitcast.7, bf16[64,512]{1,0:T(8,128)(2,1)} %w1.1, f32[1,512]{1,0:T(1,128)} %bitcast.8, bf16[512,512]{1,0:T(8,128)(2,1)} %w2.1, ...), custom_call_target="tpu_custom_call" | custom-call | tf_op jit(solution)/shard_map/pallas_call | solution.py:259
  42.4 1.6 %shard_map.123 = (f32[64,64]{1,0:T(8,128)}, f32[64,512]{1,0:T(8,128)}) custom-call(f32[64,64]{1,0:T(8,128)} %get-tuple-element.6.rin, f32[64,512]{1,0:T(8,128)} %get-tuple-element.7.cin, f32[1]{0:T(128)S(6)} %copy.13.sig), custom_call_target="tpu_custom_call" | custom-call | tf_op jit(solution)/shard_map/pallas_call | solution.py:299

commit v5 on v4

--- a/solution.py
+++ b/solution.py
@@ -19,7 +19,7 @@
 
 
 def kernel(
-    rp, rv, cp, cv, w1, b1h, w2, b2h, w3, ardh,
+    rp, rv, cp, cv, w1, b1h, w2, b2h, w3, ardh, sig,
     rout, cout,
     w1v, w2v, w3v, b1, b2, ard, rpv, rvv, xr, xo, xc, rf, fc, vrt, vct, rn, cn, pt, oc, orr,
     rsend, rrecv, csend, crecv,
@@ -232,24 +232,21 @@
     send_rows(1)
     send_cols(4)
 
+    scale = sig[0]
     arrive(row_out)
     total = rsend[0].astype(F32)
     for n in range(1, 32):
         total += rrecv[n].astype(F32)
+    total = total * scale
     rout[0:32, :] = total[:, 0:64]
     rout[32:64, :] = total[:, 64:128]
     arrive(col_out)
     total = csend[:, 0:512].astype(F32)
     for n in range(1, 8):
         total += crecv[n].astype(F32)
-    cout[...] = total
+    cout[...] = total * scale
     for c in sent:
         c.wait_send()
-
-
-def finish(rin, cin, sig, rout, cout):
-    rout[...] = rin[...] * sig[0]
-    cout[...] = cin[...] * sig[0]
 
 
 def body(rp, cp, rv, cv, w1, b1, w2, b2, w3, ard, sig):
@@ -259,7 +256,7 @@
     rows, cols = pl.pallas_call(
         kernel,
         out_shape=(jax.ShapeDtypeStruct((64, 64), F32), jax.ShapeDtypeStruct((64, 512), F32)),
-        in_specs=[away] * 10,
+        in_specs=[away] * 10 + [pl.BlockSpec(memory_space=pltpu.SMEM)],
         out_specs=(vmem, vmem),
         scratch_shapes=[
             pltpu.VMEM((128, 512), BF16),
@@ -290,18 +287,18 @@
             dma((12,)), dma((12,)), dma((32,)), dma((32,)), dma((8,)), dma((8,)),
         ],
         compiler_params=pltpu.CompilerParams(
-            collective_id=0, has_side_effects=True, vmem_limit_bytes=62 * 2**20
+            collective_id=0, has_side_effects=True, vmem_limit_bytes=40 * 2**20
         ),
     )(
-        rp, rv, cp.T, cv.T, w1, b1.reshape(1, -1), w2, b2.reshape(1, -1), w3,
-        ard.reshape(1, -1),
+        *(
+            pltpu.with_memory_space_constraint(a, pltpu.HBM)
+            for a in (
+                rp, rv, cp.T, cv.T, w1, b1.reshape(1, -1), w2, b2.reshape(1, -1), w3,
+                ard.reshape(1, -1),
+            )
+        ),
+        sig,
     )
-    rows, cols = pl.pallas_call(
-        finish,
-        out_shape=(jax.ShapeDtypeStruct((64, 64), F32), jax.ShapeDtypeStruct((64, 512), F32)),
-        in_specs=[vmem, vmem, pl.BlockSpec(memory_space=pltpu.SMEM)],
-        out_specs=(vmem, vmem),
-    )(rows, cols, sig)
     return (rows, cols.T)
 
 

time: 44.2 us -> 43.2 us (0.977)
  Pallas kernels: 42.7 us -> 40.5 us
  local copies, waits for them, and re-layouts: 0 us -> 1.27 us
    pallas_call x1 -> x0, Pallas kernels: 1.6 us -> none  [body(): pl.pallas_call(finish, out_shape=(jax.ShapeDtypeStruct((64, 64), F32), ja...]
    unnamed x0 -> x2, local copies, waits for them, and re-layouts: none -> 1.27 us
    pallas_call x1, Pallas kernels: 41.1 us -> 40.5 us  [body(): pl.pallas_call(kernel, out_shape=(jax.ShapeDtypeStruct((64, 64), F32), ja...]
where the time goes in v5:
time: 43.2 us; the launch traced here: 43.1 us
  Pallas kernels  40.5 us (94%)
  between operations  1.29 us (3%)
  local copies, waits for them, and re-layouts  1.27 us (3%)
    pallas_call x1, Pallas kernels, body(): pl.pallas_call(kernel, out_shape=(jax.ShapeDtypeStruct((64, 64), F32), ja...  40.5 us
    unnamed x2, local copies, waits for them, and re-layouts  1.27 us

profile of v5, /device:TPU:1, one launch (start us, length us, event | category | flops | bytes accessed | tf_op | source)
XLA Modules:
  0.0 43.1 jit_solution(14355677161764667604)
XLA Ops:
  1.3 40.5 %shard_map.122 = (f32[64,64]{1,0:T(8,128)S(1)}, f32[64,512]{1,0:T(8,128)S(1)}) custom-call(bf16[64,64]{1,0:T(8,128)(2,1)} %rp.1, bf16[64,64]{1,0:T(8,128)(2,1)} %rv.1, bf16[64,512]{1,0:T(8,128)(2,1)} %bitcast.7, bf16[64,512]{1,0:T(8,128)(2,1)} %bitcast.8, bf16[64,512]{1,0:T(8,128)(2,1)} %w1.1, f32[1,512]{1,0:T(1,128)} %bitcast.9, bf16[512,512]{1,0:T(8,128)(2,1)} %w2.1, ...), custom_call_target="tpu_custom_call" | custom-call | tf_op jit(solution)/shard_map/pallas_call | solution.py:256
  41.8 0.6 %copy.16 = f32[64,64]{1,0:T(8,128)} copy(f32[64,64]{1,0:T(8,128)S(1)} %get-tuple-element.8) | data formatting | bytes 32768
  42.4 0.7 %copy.17 = f32[512,64]{0,1:T(8,128)} copy(f32[512,64]{0,1:T(8,128)S(1)} %bitcast.6) | data formatting | bytes 262144

commit v6 on v5

--- a/solution.py
+++ b/solution.py
@@ -207,8 +207,7 @@
     embed_cols(512, 1536)
     last = share_cols(3)
     arrive(partner)
-    panel(0, 1536, 2048)
-    panel(0, 2048, 3584)
+    panel(0, 1536, 3584)
     arrive(last)
     arrive(ys)
     panel(0, 3584, 4096)
@@ -223,14 +222,12 @@
     panel(1, 0, 2048)
     send_cols(3, 2, 1, 0)
     panel(2, 2048, 4096)
+    send_rows(2)
     panel(1, 3072, 4096)
-    send_rows(2)
     send_cols(7, 6)
-    panel(1, 2560, 3072)
-    send_cols(5)
-    panel(1, 2048, 2560)
+    panel(1, 2048, 3072)
     send_rows(1)
-    send_cols(4)
+    send_cols(5, 4)
 
     scale = sig[0]
     arrive(row_out)

time: 43.2 us -> 43 us (level)
  no operation moved by 1% of the time
where the time goes in v6:
time: 43 us; the launch traced here: 42.9 us
  Pallas kernels  40.3 us (94%)
  between operations  1.29 us (3%)
  local copies, waits for them, and re-layouts  1.27 us (3%)
    pallas_call x1, Pallas kernels, body(): pl.pallas_call(kernel, out_shape=(jax.ShapeDtypeStruct((64, 64), F32), ja...  40.3 us
    unnamed x2, local copies, waits for them, and re-layouts  1.27 us

profile of v6, /device:TPU:1, one launch (start us, length us, event | category | flops | bytes accessed | tf_op | source)
XLA Modules:
  0.0 42.9 jit_solution(7182950050377523204)
XLA Ops:
  1.3 40.3 %shard_map.122 = (f32[64,64]{1,0:T(8,128)S(1)}, f32[64,512]{1,0:T(8,128)S(1)}) custom-call(bf16[64,64]{1,0:T(8,128)(2,1)} %rp.1, bf16[64,64]{1,0:T(8,128)(2,1)} %rv.1, bf16[64,512]{1,0:T(8,128)(2,1)} %bitcast.7, bf16[64,512]{1,0:T(8,128)(2,1)} %bitcast.8, bf16[64,512]{1,0:T(8,128)(2,1)} %w1.1, f32[1,512]{1,0:T(1,128)} %bitcast.9, bf16[512,512]{1,0:T(8,128)(2,1)} %w2.1, ...), custom_call_target="tpu_custom_call" | custom-call | tf_op jit(solution)/shard_map/pallas_call | solution.py:253
  41.6 0.6 %copy.16 = f32[64,64]{1,0:T(8,128)} copy(f32[64,64]{1,0:T(8,128)S(1)} %get-tuple-element.8) | data formatting | bytes 32768
  42.2 0.7 %copy.17 = f32[512,64]{0,1:T(8,128)} copy(f32[512,64]{0,1:T(8,128)S(1)} %bitcast.6) | data formatting | bytes 262144
